TPU v7x, 128 devices: a whole 4x4x4 slice. The times are simulated.
128 devices in a mesh: dp: 2 (over core), seq: 4 (over x), tensor: 16 (over y, z).
Axes of the slice: x: 4, y: 4, z: 4, core: 2. Of those that a mesh axis runs over, the one named last changes fastest.
Arguments:
- tokens: bfloat16 [16384, 4096], P(('dp', 'seq', 'tensor')), may hold values from -6 to 6
- cotangent: bfloat16 [16384, 14336], P(('dp', 'seq', 'tensor')), may hold values from -0.046875 to 0.046875
- master: bfloat16 [8, 336, 128, 128], P(None, 'tensor'), as said below
- block_ids: int32 [8, 336], P(None, 'tensor'), may hold values from 0 to 223, as said below
- live_count: int32 [8, 16], P(None, 'tensor'), may hold values from 1 to 21, as said below
Outputs:
- outputs: bfloat16 [16384, 14336], P(('dp', 'seq', 'tensor'))
- w_grad: float32 [8, 336, 128, 128], P(('dp', 'seq'), 'tensor')
Inputs may be any that keep to these rules, and one draw needn't show every extreme that they name: Within each group t the 168 entries block_ids[:, t * 21 : (t + 1) * 21] are distinct. `live_count`: in every group one owner uses all 21 slots. `master`: in every block one entry has the largest magnitude, and no entry of a block, divided by that magnitude over 7, lies within 0.1 of a half-integer.
All inputs are finite; a program needn't handle non-finite values. Where the computation divides by a largest or mean magnitude, that divisor is 1e-20 or more.
Results may differ from a plain program's by a relative error of at most 0.005.
Values may be sent and summed in bfloat16 or wider, within the bound.
A program may use at most 192 MiB of HBM per device.

v0:
```python
import jax
import jax.numpy as jnp
from jax import lax
from jax.sharding import PartitionSpec as P

BS = 128


def fake_quant(master, live_mask):
    master_wide = master.astype(jnp.float32)
    block_peak = jnp.max(jnp.abs(master_wide), axis=(-2, -1), keepdims=True) + 1e-06
    levels = jnp.floor(master_wide * (7.0 / block_peak) + 0.5)
    return (levels * (block_peak / 7.0) * live_mask[..., None, None]).astype(jnp.bfloat16)


def assemble(quantized, slot_ids, row_blocks, col_blocks):
    total_slots = quantized.shape[0]
    block_numbers = jnp.arange(row_blocks * col_blocks, dtype=jnp.int32)
    slot_numbers = jnp.arange(1, total_slots + 1, dtype=jnp.int32)
    matches = (slot_ids[:, None] == block_numbers[None, :]).astype(jnp.int32)
    slot_of_block = jnp.sum(matches * slot_numbers[:, None], axis=0)
    padded = jnp.concatenate([jnp.zeros((1, BS, BS), jnp.bfloat16), quantized], axis=0)
    placed = jnp.take(padded, slot_of_block, axis=0).reshape(row_blocks, col_blocks, BS, BS)
    return placed.transpose(0, 2, 1, 3).reshape(row_blocks * BS, col_blocks * BS)


def dense_gradient(token_rows, grad_rows):
    return lax.dot_general(
        token_rows, grad_rows, (((0,), (0,)), ((), ())), preferred_element_type=jnp.float32
    )


def pick_blocks(full_grad, slot_ids, row_blocks, col_blocks):
    grid_blocks = full_grad.reshape(row_blocks, BS, col_blocks, BS).transpose(0, 2, 1, 3)
    grid_blocks = grid_blocks.reshape(row_blocks * col_blocks, BS, BS)
    return jnp.take(grid_blocks, slot_ids, axis=0)


def shards(tokens, cotangent, master, block_ids, live_count):
    owners, slots = block_ids.shape
    groups = lax.axis_size("tensor")
    live_mask = (jnp.arange(slots, dtype=jnp.int32)[None, :] < live_count).astype(jnp.float32)
    quantized = fake_quant(master, live_mask).reshape(owners * slots, BS, BS)
    slot_ids = block_ids.reshape(owners * slots)
    row_blocks = tokens.shape[1] // BS
    col_blocks = cotangent.shape[1] // (BS * groups)
    dense_weight = assemble(quantized, slot_ids, row_blocks, col_blocks)
    grads_local = lax.all_to_all(cotangent, "tensor", split_axis=1, concat_axis=0, tiled=True)
    gathered = lax.all_gather(tokens, "tensor", axis=0, tiled=True)
    results = jnp.dot(gathered, dense_weight, preferred_element_type=jnp.float32)
    full_grad = dense_gradient(gathered, grads_local)
    outputs = lax.all_to_all(
        results.astype(jnp.bfloat16), "tensor", split_axis=0, concat_axis=1, tiled=True
    )
    partial_value = pick_blocks(full_grad, slot_ids, row_blocks, col_blocks)
    partial_value = (partial_value * live_mask.reshape(owners * slots)[:, None, None]).reshape(
        owners, slots, BS, BS
    )
    w_grad = lax.psum_scatter(partial_value, ("dp", "seq"), scatter_dimension=0, tiled=True)
    return (outputs, w_grad)


def solution(mesh):
    return jax.shard_map(
        shards,
        mesh=mesh,
        in_specs=(
            P(("dp", "seq", "tensor"), None),
            P(("dp", "seq", "tensor"), None),
            P(None, "tensor", None, None),
            P(None, "tensor"),
            P(None, "tensor"),
        ),
        out_specs=(P(("dp", "seq", "tensor"), None), P(("dp", "seq"), "tensor", None, None)),
        check_vma=False,
    )
```

profile of v0, /device:TPU:1, one launch (start us, length us, event | category | flops | bytes accessed | tf_op | source)
XLA Modules:
  0.0 369.7 jit_solution(11243594162319001183)
XLA Ops:
  7.2 0.0 all-gather.2.cloned.1.call-start
  7.2 0.7 all-gather.2.cloned.1.call-update
  7.9 6.1 %copy.33 = bf16[128,14336]{0,1:T(8,128)(2,1)} copy(bf16[128,14336]{1,0:T(8,128)(2,1)} %param.6) | data formatting | bytes 7340032 | tf_op args[1]
  13.9 0.0 copy-start
  13.9 0.0 copy-start.1
  14.0 6.1 %copy.34 = bf16[128,16,896]{2,0,1:T(8,128)(2,1)} copy(bf16[128,16,896]{0,2,1:T(8,128)(2,1)} %bitcast.55) | data formatting | bytes 7340032 | tf_op jit(solution)/shard_map/all_to_all | solution.py:48
  20.1 8.6 %all-to-all-start.1 = ((bf16[128,16,896]{2,0,1:T(8,128)(2,1)}), bf16[128,16,896]{2,0,1:T(8,128)(2,1)}, u32[]{:S(2)}, u32[]{:S(2)}) async-start(bf16[128,16,896]{2,0,1:T(8,128)(2,1)} %copy.34), calls=%async_computation.1 | async-start | bytes 7340032 | tf_op jit(solution)/shard_map/all_to_all | solution.py:48
  28.7 0.0 reduce-scatter.2.cloned.1.call-start
  28.8 0.0 copy-done
  28.8 0.1 reshape.139
  28.9 0.0 copy-done.1
  28.9 0.1 fusion.11
  29.0 4.0 %fusion = f32[8,21]{1,0:T(8,128)S(1)} fusion(bf16[8,21,128,128]{3,2,1,0:T(8,128)(2,1)} %param.7), kind=kLoop, calls=%fused_computation.4 | loop fusion | flops 8257368 | bytes 5505696 | tf_op jit(solution)/shard_map/reduce_max | solution.py:11
  32.9 68.2 %all-to-all-done.1 = bf16[128,16,896]{2,0,1:T(8,128)(2,1)} async-done(((bf16[128,16,896]{2,0,1:T(8,128)(2,1)}), bf16[128,16,896]{2,0,1:T(8,128)(2,1)}, u32[]{:S(2)}, u32[]{:S(2)}) %all-to-all-start.1) | async-done | bytes 3670048 | tf_op jit(solution)/shard_map/all_to_all | solution.py:48
  101.2 6.1 %copy.35 = bf16[2048,896]{0,1:T(8,128)(2,1)} copy(bf16[2048,896]{1,0:T(8,128)(2,1)} %bitcast.15) | data formatting | bytes 7340032 | tf_op jit(solution)/shard_map/all_to_all | solution.py:48
  107.2 57.2 %all-gather.2.cloned.1.call-done = bf16[2048,4096]{1,0:T(8,128)(2,1)} async-done(((bf16[128,4096]{1,0:T(8,128)(2,1)}), bf16[2048,4096]{1,0:T(8,128)(2,1)}) %all-gather.2.cloned.1.call-update) | async-done | bytes 16777232 | tf_op jit(solution)/shard_map/all_gather | solution.py:49
  164.5 22.5 %copy.32 = bf16[4096,2048]{1,0:T(8,128)(2,1)} copy(bf16[4096,2048]{0,1:T(8,128)(2,1)} %bitcast.51) | data formatting | bytes 33554432 | tf_op jit(solution)/shard_map/dot_general | solution.py:28
  187.0 23.3 %fusion.12 = f32[32,128,7,128]{3,1,2,0:T(8,128)} fusion(bf16[32,128,2048,1]{2,1,3,0:T(8,128)(2,1)} %bitcast.52, bf16[7,128,2048,1]{2,1,0,3:T(8,128)(2,1)} %bitcast.58), kind=kOutput, calls=%fused_computation.32 | convolution fusion | flops 15032385536 | bytes 35127296 | tf_op jit(solution)/shard_map/dot_general | solution.py:28
  210.3 15.5 %gather_fusion.1 = f32[168,128,128]{2,1,0:T(8,128)} fusion(f32[224,128,128]{2,1,0:T(8,128)} %bitcast.56, s32[1024]{0:T(1024)S(1)} %pad_clamp_fusion), kind=kCustom, calls=%fused_computation.1 | custom fusion | bytes 22020768 | tf_op jit(solution)/shard_map/jit(_take)/gather | solution.py:36
  225.8 14.1 %select_multiply_fusion = (f32[8,21,128,128]{3,2,1,0:T(8,128)}, bf16[8,21,128,128]{3,2,1,0:T(8,128)(2,1)}) fusion(f32[8,21,128,128]{3,2,1,0:T(8,128)} %bitcast.48, f32[8,21]{1,0:T(8,128)S(1)} %get-tuple-element.12, pred[8,21]{1,0:T(8,128)(4,1)S(1)} %get-tuple-element.13, f32[8,21]{1,0:T(8,128)S(1)} %get-tuple-element.11, f32[8,21]{1,0:T(8,128)S(1)} %get-tuple-element.10, ...), kind=kLoop, calls=%fused_computation.10 | loop fusion | flops 24772608 | bytes 33032328 | tf_op jit(solution)/shard_map/mul | solution.py:56
  239.9 0.0 reduce-scatter.2.cloned.1.call-update
  240.0 0.1 eq.15
  240.0 0.1 select_reduce_fusion
  240.2 0.1 reduce_sum.14
  240.3 7.2 %concatenate.3 = bf16[169,128,128]{2,1,0:T(8,128)(2,1)} pad(bf16[168,128,128]{2,1,0:T(8,128)(2,1)} %bitcast.50, bf16[]{:T(256)} %constant.42.clone.1), padding=1_0x0_0x0_0 | pad | bytes 11042818 | tf_op jit(solution)/shard_map/concatenate | solution.py:22
  247.5 11.1 %gather_fusion = bf16[224,128,128]{2,1,0:T(8,128)(2,1)} fusion(bf16[169,128,128]{2,1,0:T(8,128)(2,1)} %concatenate.3, s32[1024]{0:T(1024)S(1)} %pad_clamp_fusion.1), kind=kCustom, calls=%fused_computation | custom fusion | bytes 14680960 | tf_op jit(solution)/shard_map/jit(_take)/gather | solution.py:23
  258.6 6.8 %select_bitcast_fusion = bf16[32,128,7,128]{3,1,2,0:T(8,128)(2,1)} fusion(bf16[32,7,128,128]{3,2,1,0:T(8,128)(2,1)} %bitcast.49, pred[32,7]{1,0:T(8,128)(4,1)S(1)} %compare_and_fusion), kind=kLoop, calls=%fused_computation.14 | loop fusion | flops 3670016 | bytes 14680288 | tf_op jit(solution)/shard_map/transpose | solution.py:24
  265.4 12.2 %copy.30 = bf16[32,128,7,128]{1,0,3,2:T(8,128)(2,1)} copy(bf16[32,128,7,128]{3,1,2,0:T(8,128)(2,1)} %select_bitcast_fusion) | data formatting | bytes 14680064 | tf_op jit(solution)/shard_map/transpose | solution.py:24
  277.6 20.9 %convert_bitcast_fusion = bf16[112,16,8,128]{3,2,1,0:T(8,128)(2,1)S(1)} fusion(bf16[2048,4096]{1,0:T(8,128)(2,1)} %all-gather.2.cloned.1.call-done, bf16[112,8,32,128]{3,2,1,0:T(8,128)(2,1)} %bitcast.57), kind=kOutput, calls=%fused_computation.16 | convolution fusion | flops 15034220544 | bytes 27787264 | tf_op jit(solution)/shard_map/dot_general | solution.py:50
  298.5 0.9 copy.47
  299.5 55.9 %all_to_all.38 = bf16[16,128,896]{1,2,0:T(8,128)(2,1)} all-to-all(bf16[16,128,896]{1,2,0:T(8,128)(2,1)S(1)} %bitcast.53), channel_id=1, replica_groups=mesh['dp'=2,'seq'=4,'tensor'=16] {'tensor'}, dimensions={0} | all-to-all | bytes 7340032 | tf_op jit(solution)/shard_map/all_to_all | solution.py:52
  355.3 6.1 %copy.36 = bf16[128,14336]{1,0:T(8,128)(2,1)} copy(bf16[128,14336]{0,1:T(8,128)(2,1)} %bitcast.54) | data formatting | bytes 7340032
  361.5 1.4 reduce-scatter.2.cloned.1.call-done
  (7 shorter events, 0.0 us)
Async XLA Ops:
  7.2 157.3 %all-gather.2.cloned.1.call-start = ((), (), s32[]{:S(2)}) async-start(), calls=%async_computation.3 | async-start | bytes 17825792 | tf_op jit(solution)/shard_map/all_gather | solution.py:49
  13.9 14.8 %copy-start = (s32[8,21]{1,0:T(8,128)S(1)}, s32[8,21]{1,0:T(8,128)}, u32[]{:S(2)}) copy-start(s32[8,21]{1,0:T(8,128)} %param.8) | copy-start | bytes 2020
  13.9 14.9 %copy-start.1 = (s32[8,1]{0,1:T(1,128)S(1)}, s32[8,1]{0,1:T(1,128)}, u32[]{:S(2)}) copy-start(s32[8,1]{0,1:T(1,128)} %param.9) | copy-start | bytes 100
  20.1 81.1 %all-to-all-start.1 = ((bf16[128,16,896]{2,0,1:T(8,128)(2,1)}), bf16[128,16,896]{2,0,1:T(8,128)(2,1)}, u32[]{:S(2)}, u32[]{:S(2)}) async-start(bf16[128,16,896]{2,0,1:T(8,128)(2,1)} %copy.34), calls=%async_computation.1 | async-start | bytes 7340032 | tf_op jit(solution)/shard_map/all_to_all | solution.py:48
  28.7 334.1 %reduce-scatter.2.cloned.1.call-start = ((), (), s32[]{:S(2)}) async-start(), calls=%async_computation.4 | async-start | bytes 12386304 | tf_op jit(solution)/shard_map/reduce_scatter | solution.py:59
Sparse Core Ops, SparseCore 0:
  10.1 154.2 all-gather.1
  240.1 122.7 reduce-scatter.1
where the time goes:
time: 371 us; the launch traced here: 370 us
  waiting for transfers between devices  128 us (35%)
  local copies, waits for them, and re-layouts  94.1 us (25%)
  blocking collectives  55.9 us (15%)
  matrix products  44.2 us (12%)
  other arithmetic  25.1 us (7%)
  between operations  14.1 us (4%)
  starting transfers between devices  8.72 us (2%)
    all_to_all x1, waiting for transfers between devices, shards(): lax.all_to_all(cotangent, 'tensor', split_axis=1, concat_axis=0, tiled=True)  68.2 us
    all_gather x1, waiting for transfers between devices, shards(): gathered = lax.all_gather(tokens, 'tensor', axis=0, tiled=True)  57.2 us
    all_to_all x1, blocking collectives, shards(): lax.all_to_all(results.astype(jnp.bfloat16), 'tensor', split_axis=0, conc...  55.9 us
    dot_general x1, matrix products, dense_gradient(): lax.dot_general(token_rows, grad_rows, (((0,), (0,)), ((), ())), preferre...  23.3 us
    dot_general x1, local copies, waits for them, and re-layouts, dense_gradient(): lax.dot_general(token_rows, grad_rows, (((0,), (0,)), ((), ())), preferre...  22.5 us
    dot_general x1, matrix products, shards(): jnp.dot(gathered, dense_weight, preferred_element_type=jnp.float32)  20.9 us
    gather x1, local copies, waits for them, and re-layouts, pick_blocks(): return jnp.take(grid_blocks, slot_ids, axis=0)  15.5 us
    mul x1, other arithmetic, shards(): partial_value * live_mask.reshape(owners * slots)[:, None, None]  14.1 us
  transfers between devices with their start and end apart: 3, of which 3 were waited for; matrix products, arithmetic and copies ran while one was open for 24% of the time, Pallas kernels for 0%

commit v1 on v0

--- a/solution.py
+++ b/solution.py
@@ -46,7 +46,22 @@
     col_blocks = cotangent.shape[1] // (BS * groups)
     dense_weight = assemble(quantized, slot_ids, row_blocks, col_blocks)
     grads_local = lax.all_to_all(cotangent, "tensor", split_axis=1, concat_axis=0, tiled=True)
-    gathered = lax.all_gather(tokens, "tensor", axis=0, tiled=True)
+    count, index, rows = (lax.axis_size("tensor"), lax.axis_index("tensor"), tokens.shape[0])
+    forward = [(i, (i + 1) % count) for i in range(count)]
+    behind = [(i, (i - 1) % count) for i in range(count)]
+    out = jnp.zeros((*tokens.shape[:0], count * rows, *tokens.shape[0 + 1 :]), tokens.dtype)
+    out = lax.dynamic_update_slice_in_dim(out, tokens, index * rows, axis=0)
+    from_left = from_right = tokens
+    half = count // 2
+    for step in range(1, half + 1):
+        from_left = lax.ppermute(from_left, "tensor", forward)
+        out = lax.dynamic_update_slice_in_dim(out, from_left, (index - step) % count * rows, axis=0)
+        if step < count - half:
+            from_right = lax.ppermute(from_right, "tensor", behind)
+            out = lax.dynamic_update_slice_in_dim(
+                out, from_right, (index + step) % count * rows, axis=0
+            )
+    gathered = out
     results = jnp.dot(gathered, dense_weight, preferred_element_type=jnp.float32)
     full_grad = dense_gradient(gathered, grads_local)
     outputs = lax.all_to_all(

time: 371 us -> 437 us (1.18)
  starting transfers between devices: 8.72 us -> 43.5 us
  waiting for transfers between devices: 128 us -> 149 us
  local copies, waits for them, and re-layouts: 94.1 us -> 112 us
  blocking collectives: 55.9 us -> 41.2 us
  matrix products: 44.2 us -> 49.8 us
    ppermute x0 -> x15, waiting for transfers between devices: none -> 139 us  [the longest x8 122 us: shards(): from_left = lax.ppermute(from_left, 'tensor', forward)]
    all_to_all x1, waiting for transfers between devices: 68.2 us -> 0.01 us  [shards(): lax.all_to_all(cotangent, 'tensor', split_axis=1, concat_axis=0, tiled=True)]
    all_gather x1 -> x0, waiting for transfers between devices: 57.2 us -> none  [shards(): gathered = lax.all_gather(tokens, 'tensor', axis=0, tiled=True)]
    ppermute x0 -> x15, starting transfers between devices: none -> 39 us  [the longest x7 36.5 us: shards(): from_right = lax.ppermute(from_right, 'tensor', behind)]
    dot_general x1 -> x0, local copies, waits for them, and re-layouts: 22.5 us -> none  [dense_gradient(): lax.dot_general(token_rows, grad_rows, (((0,), (0,)), ((), ())), preferre...]
    ppermute x0 -> x15, local copies, waits for them, and re-layouts: none -> 20.3 us  [the longest x8 12.9 us: shards(): from_left = lax.ppermute(from_left, 'tensor', forward)]
    dynamic_update_slice x0 -> x16, local copies, waits for them, and re-layouts: none -> 18 us  [the longest x8 8.96 us: shards(): lax.dynamic_update_slice_in_dim(out, from_left, (index - step) % count *...]
    all_to_all x1, blocking collectives: 55.9 us -> 41.2 us  [shards(): lax.all_to_all(results.astype(jnp.bfloat16), 'tensor', split_axis=0, conc...]
  transfers between devices with their start and end apart: 3 -> 17, of which waited for: 3 -> 12; matrix products, arithmetic and copies ran while one was open for 24% -> 30% of each run, Pallas kernels for 0% -> 0%
where the time goes in v1:
time: 437 us; the launch traced here: 435 us
  waiting for transfers between devices  149 us (34%)
  local copies, waits for them, and re-layouts  112 us (26%)
  matrix products  49.8 us (11%)
  starting transfers between devices  43.5 us (10%)
  blocking collectives  41.2 us (9%)
  other arithmetic  25 us (6%)
  between operations  14.6 us (3%)
    ppermute x8, waiting for transfers between devices, shards(): from_left = lax.ppermute(from_left, 'tensor', forward)  122 us
    all_to_all x1, blocking collectives, shards(): lax.all_to_all(results.astype(jnp.bfloat16), 'tensor', split_axis=0, conc...  41.2 us
    ppermute x7, starting transfers between devices, shards(): from_right = lax.ppermute(from_right, 'tensor', behind)  36.5 us
    dot_general x1, matrix products, shards(): jnp.dot(gathered, dense_weight, preferred_element_type=jnp.float32)  26.5 us
    dot_general x1, matrix products, dense_gradient(): lax.dot_general(token_rows, grad_rows, (((0,), (0,)), ((), ())), preferre...  23.3 us
    ppermute x7, waiting for transfers between devices, shards(): from_right = lax.ppermute(from_right, 'tensor', behind)  16.8 us
    gather x1, local copies, waits for them, and re-layouts, pick_blocks(): return jnp.take(grid_blocks, slot_ids, axis=0)  15.4 us
    mul x1, other arithmetic, shards(): partial_value * live_mask.reshape(owners * slots)[:, None, None]  14.1 us
  transfers between devices with their start and end apart: 17, of which 12 were waited for; matrix products, arithmetic and copies ran while one was open for 30% of the time, Pallas kernels for 0%

profile of v1, /device:TPU:1, one launch (start us, length us, event | category | flops | bytes accessed | tf_op | source)
XLA Modules:
  0.0 435.3 jit_solution(12131055936775116812)
XLA Ops:
  7.2 2.5 collective-permute-start
  9.7 4.7 %collective-permute-start.1 = (bf16[128,4096]{1,0:T(8,128)(2,1)}, bf16[128,4096]{1,0:T(8,128)(2,1)S(1)}, u32[]{:S(2)}, u32[]{:S(2)}) collective-permute-start(bf16[128,4096]{1,0:T(8,128)(2,1)} %param.5), channel_id=1, source_target_pairs={{0,15},{1,0},{2,1},{3,2},{4,3},{5,4},{6,5},{7,6},{8,7},{9,8},{10,9... | collective-permute-start | bytes 3145736 | tf_op jit(solution)/shard_map/ppermute | solution.py:60
  14.4 23.1 %collective-permute-done = bf16[128,4096]{1,0:T(8,128)(2,1)} collective-permute-done((bf16[128,4096]{1,0:T(8,128)(2,1)}, bf16[128,4096]{1,0:T(8,128)(2,1)}, u32[]{:S(2)}, u32[]{:S(2)}) %collective-permute-start) | collective-permute-done | bytes 1048608 | tf_op jit(solution)/shard_map/ppermute | solution.py:57
  37.5 4.8 %collective-permute-start.3 = (bf16[128,4096]{1,0:T(8,128)(2,1)S(1)}, bf16[128,4096]{1,0:T(8,128)(2,1)S(1)}, u32[]{:S(2)}, u32[]{:S(2)}) collective-permute-start(bf16[128,4096]{1,0:T(8,128)(2,1)S(1)} %collective-permute-done.1), channel_id=1, source_target_pairs={{0,15},{1,0},{2,1},{3,2},{4,3},{5,4},{6,5},{7,6},{8,7},{9,8},{10,9... | collective-permute-start | bytes 3145736 | tf_op jit(solution)/shard_map/ppermute | solution.py:60
  42.3 6.0 %copy.127 = bf16[128,14336]{0,1:T(8,128)(2,1)} copy(bf16[128,14336]{1,0:T(8,128)(2,1)} %param.6) | data formatting | bytes 7340032 | tf_op args[1]
  48.3 6.1 %copy.128 = bf16[128,16,896]{2,0,1:T(8,128)(2,1)} copy(bf16[128,16,896]{0,2,1:T(8,128)(2,1)} %bitcast.48) | data formatting | bytes 7340032 | tf_op jit(solution)/shard_map/all_to_all | solution.py:48
  54.4 4.5 %all-to-all-start.1 = ((bf16[128,16,896]{2,0,1:T(8,128)(2,1)}), bf16[128,16,896]{2,0,1:T(8,128)(2,1)}, u32[]{:S(2)}, u32[]{:S(2)}) async-start(bf16[128,16,896]{2,0,1:T(8,128)(2,1)} %copy.128), calls=%async_computation.1 | async-start | bytes 7340032 | tf_op jit(solution)/shard_map/all_to_all | solution.py:48
  59.1 3.9 fusion
  63.0 2.6 collective-permute-done.2
  65.5 6.3 %collective-permute-done.3 = bf16[128,4096]{1,0:T(8,128)(2,1)S(1)} collective-permute-done((bf16[128,4096]{1,0:T(8,128)(2,1)S(1)}, bf16[128,4096]{1,0:T(8,128)(2,1)S(1)}, u32[]{:S(2)}, u32[]{:S(2)}) %collective-permute-start.3) | collective-permute-done | bytes 1048608 | tf_op jit(solution)/shard_map/ppermute | solution.py:60
  71.8 6.7 %collective-permute-start.5 = (bf16[128,4096]{1,0:T(8,128)(2,1)S(1)}, bf16[128,4096]{1,0:T(8,128)(2,1)}, u32[]{:S(2)}, u32[]{:S(2)}) collective-permute-start(bf16[128,4096]{1,0:T(8,128)(2,1)S(1)} %collective-permute-done.3), channel_id=1, source_target_pairs={{0,15},{1,0},{2,1},{3,2},{4,3},{5,4},{6,5},{7,6},{8,7},{9,8},{10,9... | collective-permute-start | bytes 3145736 | tf_op jit(solution)/shard_map/ppermute | solution.py:60
  78.6 0.7 copy.108
  79.6 6.0 %broadcast_in_dim.29 = bf16[2048,4096]{0,1:T(8,128)(2,1)} broadcast(bf16[]{:T(256)} %constant.121.clone.1), dimensions={} | broadcast | bytes 16777218 | tf_op jit(solution)/shard_map/broadcast_in_dim | solution.py:52
  85.6 1.1 constant_dynamic-update-slice_fusion.15
  86.7 43.4 %collective-permute-done.4 = bf16[128,4096]{1,0:T(8,128)(2,1)} collective-permute-done((bf16[128,4096]{1,0:T(8,128)(2,1)}, bf16[128,4096]{1,0:T(8,128)(2,1)}, u32[]{:S(2)}, u32[]{:S(2)}) %collective-permute-start.4) | collective-permute-done | bytes 1048608 | tf_op jit(solution)/shard_map/ppermute | solution.py:57
  130.2 1.6 copy.109
  131.8 4.8 %collective-permute-start.7 = (bf16[128,4096]{1,0:T(8,128)(2,1)}, bf16[128,4096]{1,0:T(8,128)(2,1)}, u32[]{:S(2)}, u32[]{:S(2)}) collective-permute-start(bf16[128,4096]{1,0:T(8,128)(2,1)} %collective-permute-done.5), channel_id=1, source_target_pairs={{0,15},{1,0},{2,1},{3,2},{4,3},{5,4},{6,5},{7,6},{8,7},{9,8},{10,9... | collective-permute-start | bytes 3145736 | tf_op jit(solution)/shard_map/ppermute | solution.py:60
  136.6 1.1 constant_dynamic-update-slice_fusion.14
  138.4 1.1 constant_dynamic-update-slice_fusion.13
  139.6 1.6 copy.111
  141.2 15.7 %collective-permute-done.6 = bf16[128,4096]{1,0:T(8,128)(2,1)} collective-permute-done((bf16[128,4096]{1,0:T(8,128)(2,1)}, bf16[128,4096]{1,0:T(8,128)(2,1)}, u32[]{:S(2)}, u32[]{:S(2)}) %collective-permute-start.6) | collective-permute-done | bytes 1048608 | tf_op jit(solution)/shard_map/ppermute | solution.py:57
  156.9 1.1 constant_dynamic-update-slice_fusion.12
  158.6 4.9 %collective-permute-start.9 = (bf16[128,4096]{1,0:T(8,128)(2,1)}, bf16[128,4096]{1,0:T(8,128)(2,1)S(1)}, u32[]{:S(2)}, u32[]{:S(2)}) collective-permute-start(bf16[128,4096]{1,0:T(8,128)(2,1)} %collective-permute-done.7), channel_id=1, source_target_pairs={{0,15},{1,0},{2,1},{3,2},{4,3},{5,4},{6,5},{7,6},{8,7},{9,8},{10,9... | collective-permute-start | bytes 3145736 | tf_op jit(solution)/shard_map/ppermute | solution.py:60
  163.5 1.2 constant_dynamic-update-slice_fusion.11
  164.7 1.6 copy.113
  166.3 1.6 copy.114
  167.9 1.1 constant_dynamic-update-slice_fusion.10
  169.0 13.7 %collective-permute-done.8 = bf16[128,4096]{1,0:T(8,128)(2,1)} collective-permute-done((bf16[128,4096]{1,0:T(8,128)(2,1)}, bf16[128,4096]{1,0:T(8,128)(2,1)}, u32[]{:S(2)}, u32[]{:S(2)}) %collective-permute-start.8) | collective-permute-done | bytes 1048608 | tf_op jit(solution)/shard_map/ppermute | solution.py:57
  182.7 1.1 constant_dynamic-update-slice_fusion.9
  183.8 6.0 %copy.129 = bf16[2048,896]{0,1:T(8,128)(2,1)} copy(bf16[2048,896]{1,0:T(8,128)(2,1)} %bitcast.14) | data formatting | bytes 7340032 | tf_op jit(solution)/shard_map/all_to_all | solution.py:48
  189.8 1.6 copy.115
  191.4 4.9 %collective-permute-start.11 = (bf16[128,4096]{1,0:T(8,128)(2,1)S(1)}, bf16[128,4096]{1,0:T(8,128)(2,1)}, u32[]{:S(2)}, u32[]{:S(2)}) collective-permute-start(bf16[128,4096]{1,0:T(8,128)(2,1)S(1)} %collective-permute-done.9), channel_id=1, source_target_pairs={{0,15},{1,0},{2,1},{3,2},{4,3},{5,4},{6,5},{7,6},{8,7},{9,8},{10,9... | collective-permute-start | bytes 3145736 | tf_op jit(solution)/shard_map/ppermute | solution.py:60
  196.4 1.1 constant_dynamic-update-slice_fusion.8
  197.5 1.6 copy.116
  199.1 1.1 constant_dynamic-update-slice_fusion.7
  200.3 1.6 copy.117
  201.9 5.7 %collective-permute-done.10 = bf16[128,4096]{1,0:T(8,128)(2,1)} collective-permute-done((bf16[128,4096]{1,0:T(8,128)(2,1)}, bf16[128,4096]{1,0:T(8,128)(2,1)}, u32[]{:S(2)}, u32[]{:S(2)}) %collective-permute-start.10) | collective-permute-done | bytes 1048608 | tf_op jit(solution)/shard_map/ppermute | solution.py:57
  207.5 1.1 constant_dynamic-update-slice_fusion.6
  209.3 5.8 %collective-permute-done.11 = bf16[128,4096]{1,0:T(8,128)(2,1)} collective-permute-done((bf16[128,4096]{1,0:T(8,128)(2,1)S(1)}, bf16[128,4096]{1,0:T(8,128)(2,1)}, u32[]{:S(2)}, u32[]{:S(2)}) %collective-permute-start.11) | collective-permute-done | bytes 1048608 | tf_op jit(solution)/shard_map/ppermute | solution.py:60
  215.1 5.6 %collective-permute-start.13 = (bf16[128,4096]{1,0:T(8,128)(2,1)}, bf16[128,4096]{1,0:T(8,128)(2,1)S(1)}, u32[]{:S(2)}, u32[]{:S(2)}) collective-permute-start(bf16[128,4096]{1,0:T(8,128)(2,1)} %collective-permute-done.11), channel_id=1, source_target_pairs={{0,15},{1,0},{2,1},{3,2},{4,3},{5,4},{6,5},{7,6},{8,7},{9,8},{10,9... | collective-permute-start | bytes 3145736 | tf_op jit(solution)/shard_map/ppermute | solution.py:60
  220.7 1.1 constant_dynamic-update-slice_fusion.5
  221.9 1.6 copy.119
  223.5 1.6 copy.120
  225.1 1.1 constant_dynamic-update-slice_fusion.4
  226.2 5.3 %collective-permute-done.12 = bf16[128,4096]{1,0:T(8,128)(2,1)} collective-permute-done((bf16[128,4096]{1,0:T(8,128)(2,1)}, bf16[128,4096]{1,0:T(8,128)(2,1)}, u32[]{:S(2)}, u32[]{:S(2)}) %collective-permute-start.12) | collective-permute-done | bytes 1048608 | tf_op jit(solution)/shard_map/ppermute | solution.py:57
  231.5 1.2 constant_dynamic-update-slice_fusion.3
  232.7 1.6 copy.121
  234.3 4.6 %collective-permute-done.13 = bf16[128,4096]{1,0:T(8,128)(2,1)S(1)} collective-permute-done((bf16[128,4096]{1,0:T(8,128)(2,1)}, bf16[128,4096]{1,0:T(8,128)(2,1)S(1)}, u32[]{:S(2)}, u32[]{:S(2)}) %collective-permute-start.13) | collective-permute-done | bytes 1048608 | tf_op jit(solution)/shard_map/ppermute | solution.py:60
  239.6 1.2 constant_dynamic-update-slice_fusion.2
  240.7 1.1 constant_dynamic-update-slice_fusion.1
  241.8 12.7 %collective-permute-done.14 = bf16[128,4096]{1,0:T(8,128)(2,1)} collective-permute-done((bf16[128,4096]{1,0:T(8,128)(2,1)}, bf16[128,4096]{1,0:T(8,128)(2,1)}, u32[]{:S(2)}, u32[]{:S(2)}) %collective-permute-start.14) | collective-permute-done | bytes 1048608 | tf_op jit(solution)/shard_map/ppermute | solution.py:57
  254.5 1.6 copy.123
  256.1 1.1 constant_dynamic-update-slice_fusion
  257.3 23.3 %fusion.13 = f32[32,128,7,128]{3,1,2,0:T(8,128)} fusion(bf16[32,128,2048,1]{2,1,3,0:T(8,128)(2,1)} %bitcast.11, bf16[7,128,2048,1]{2,1,0,3:T(8,128)(2,1)} %bitcast.51), kind=kOutput, calls=%fused_computation.47 | convolution fusion | flops 15032385536 | bytes 35127296 | tf_op jit(solution)/shard_map/dot_general | solution.py:28
  280.5 15.4 %gather_fusion.1 = f32[168,128,128]{2,1,0:T(8,128)} fusion(f32[224,128,128]{2,1,0:T(8,128)} %bitcast.49, s32[1024]{0:T(1024)S(1)} %pad_clamp_fusion), kind=kCustom, calls=%fused_computation.1 | custom fusion | bytes 22020768 | tf_op jit(solution)/shard_map/jit(_take)/gather | solution.py:36
  295.9 14.1 %select_multiply_fusion = (f32[8,21,128,128]{3,2,1,0:T(8,128)}, bf16[8,21,128,128]{3,2,1,0:T(8,128)(2,1)}) fusion(f32[8,21,128,128]{3,2,1,0:T(8,128)} %bitcast.44, f32[8,21]{1,0:T(8,128)S(1)} %get-tuple-element.6, pred[8,21]{1,0:T(8,128)(4,1)S(1)} %get-tuple-element.7, f32[8,21]{1,0:T(8,128)S(1)} %get-tuple-element.5, f32[8,21]{1,0:T(8,128)S(1)} %get-tuple-element.4, ...), kind=kLoop, calls=%fused_computation.10 | loop fusion | flops 24772608 | bytes 33032328 | tf_op jit(solution)/shard_map/mul | solution.py:71
  310.4 7.2 %concatenate.3 = bf16[169,128,128]{2,1,0:T(8,128)(2,1)} pad(bf16[168,128,128]{2,1,0:T(8,128)(2,1)} %bitcast.46, bf16[]{:T(256)} %constant.121.clone.1), padding=1_0x0_0x0_0 | pad | bytes 11042818 | tf_op jit(solution)/shard_map/concatenate | solution.py:22
  317.5 11.1 %gather_fusion = bf16[224,128,128]{2,1,0:T(8,128)(2,1)} fusion(bf16[169,128,128]{2,1,0:T(8,128)(2,1)} %concatenate.3, s32[1024]{0:T(1024)S(1)} %pad_clamp_fusion.1), kind=kCustom, calls=%fused_computation | custom fusion | bytes 14680960 | tf_op jit(solution)/shard_map/jit(_take)/gather | solution.py:23
  328.6 6.8 %select_bitcast_fusion = bf16[32,128,7,128]{3,1,2,0:T(8,128)(2,1)} fusion(bf16[32,7,128,128]{3,2,1,0:T(8,128)(2,1)} %bitcast.45, pred[32,7]{1,0:T(8,128)(4,1)S(1)} %compare_and_fusion), kind=kLoop, calls=%fused_computation.14 | loop fusion | flops 3670016 | bytes 14680288 | tf_op jit(solution)/shard_map/transpose | solution.py:24
  335.5 12.2 %copy.124 = bf16[32,128,7,128]{1,0,3,2:T(8,128)(2,1)} copy(bf16[32,128,7,128]{3,1,2,0:T(8,128)(2,1)} %select_bitcast_fusion) | data formatting | bytes 14680064 | tf_op jit(solution)/shard_map/transpose | solution.py:24
  347.6 26.5 %fusion.9 = bf16[2048,896]{1,0:T(8,128)(2,1)S(1)} fusion(bf16[2048,4096]{0,1:T(8,128)(2,1)} %constant_dynamic-update-slice_fusion, bf16[112,8,32,128]{3,2,1,0:T(8,128)(2,1)} %bitcast.50), kind=kOutput, calls=%fused_computation.15 | convolution fusion | flops 15034220544 | bytes 27787264 | tf_op jit(solution)/shard_map/dot_general | solution.py:65
  374.2 41.2 %all_to_all.38 = bf16[16,128,896]{2,1,0:T(8,128)(2,1)S(1)} all-to-all(bf16[16,128,896]{2,1,0:T(8,128)(2,1)S(1)} %bitcast.53), channel_id=1, replica_groups=mesh['dp'=2,'seq'=4,'tensor'=16] {'tensor'}, dimensions={0} | all-to-all | bytes 7340032 | tf_op jit(solution)/shard_map/all_to_all | solution.py:67
  415.4 2.4 copy.132
  417.8 10.6 %reduce-scatter.2.cloned.1.call-done = f32[1,21,128,128]{3,2,1,0:T(8,128)} async-done(((f32[8,21,128,128]{3,2,1,0:T(8,128)}), f32[1,21,128,128]{3,2,1,0:T(8,128)}) %reduce-scatter.2.cloned.1.call-update) | async-done | bytes 1376272 | tf_op jit(solution)/shard_map/reduce_scatter | solution.py:74
  (40 shorter events, 3.2 us)
Async XLA Ops:
  7.2 71.4 %copy-start = (bf16[128,4096]{1,0:T(8,128)(2,1)S(1)}, bf16[128,4096]{1,0:T(8,128)(2,1)}, u32[]{:S(2)}) copy-start(bf16[128,4096]{1,0:T(8,128)(2,1)} %param.5) | copy-start | bytes 3145732
  7.2 51.8 %copy-start.3 = (s32[8,21]{1,0:T(8,128)S(1)}, s32[8,21]{1,0:T(8,128)}, u32[]{:S(2)}) copy-start(s32[8,21]{1,0:T(8,128)} %param.8) | copy-start | bytes 2020
  7.2 72.2 %copy-start.4 = (s32[8,1]{0,1:T(1,128)S(1)}, s32[8,1]{0,1:T(1,128)}, u32[]{:S(2)}) copy-start(s32[8,1]{0,1:T(1,128)} %param.9) | copy-start | bytes 100
  7.2 30.3 %collective-permute-start = (bf16[128,4096]{1,0:T(8,128)(2,1)}, bf16[128,4096]{1,0:T(8,128)(2,1)}, u32[]{:S(2)}, u32[]{:S(2)}) collective-permute-start(bf16[128,4096]{1,0:T(8,128)(2,1)} %param.5), channel_id=1, source_target_pairs={{0,1},{1,2},{2,3},{3,4},{4,5},{5,6},{6,7},{7,8},{8,9},{9,10},{10,1... | collective-permute-start | bytes 3145736 | tf_op jit(solution)/shard_map/ppermute | solution.py:57
  9.7 27.8 %collective-permute-start.1 = (bf16[128,4096]{1,0:T(8,128)(2,1)}, bf16[128,4096]{1,0:T(8,128)(2,1)S(1)}, u32[]{:S(2)}, u32[]{:S(2)}) collective-permute-start(bf16[128,4096]{1,0:T(8,128)(2,1)} %param.5), channel_id=1, source_target_pairs={{0,15},{1,0},{2,1},{3,2},{4,3},{5,4},{6,5},{7,6},{8,7},{9,8},{10,9... | collective-permute-start | bytes 3145736 | tf_op jit(solution)/shard_map/ppermute | solution.py:60
  37.5 28.0 %collective-permute-start.2 = (bf16[128,4096]{1,0:T(8,128)(2,1)}, bf16[128,4096]{1,0:T(8,128)(2,1)}, u32[]{:S(2)}, u32[]{:S(2)}) collective-permute-start(bf16[128,4096]{1,0:T(8,128)(2,1)} %collective-permute-done), channel_id=1, source_target_pairs={{0,1},{1,2},{2,3},{3,4},{4,5},{5,6},{6,7},{7,8},{8,9},{9,10},{10,1... | collective-permute-start | bytes 3145736 | tf_op jit(solution)/shard_map/ppermute | solution.py:57
  37.5 41.1 %copy-start.1 = (bf16[128,4096]{1,0:T(8,128)(2,1)}, bf16[128,4096]{1,0:T(8,128)(2,1)S(1)}, u32[]{:S(2)}) copy-start(bf16[128,4096]{1,0:T(8,128)(2,1)S(1)} %collective-permute-done.1) | copy-start | bytes 3145732
  37.5 34.3 %collective-permute-start.3 = (bf16[128,4096]{1,0:T(8,128)(2,1)S(1)}, bf16[128,4096]{1,0:T(8,128)(2,1)S(1)}, u32[]{:S(2)}, u32[]{:S(2)}) collective-permute-start(bf16[128,4096]{1,0:T(8,128)(2,1)S(1)} %collective-permute-done.1), channel_id=1, source_target_pairs={{0,15},{1,0},{2,1},{3,2},{4,3},{5,4},{6,5},{7,6},{8,7},{9,8},{10,9... | collective-permute-start | bytes 3145736 | tf_op jit(solution)/shard_map/ppermute | solution.py:60
  54.4 129.3 %all-to-all-start.1 = ((bf16[128,16,896]{2,0,1:T(8,128)(2,1)}), bf16[128,16,896]{2,0,1:T(8,128)(2,1)}, u32[]{:S(2)}, u32[]{:S(2)}) async-start(bf16[128,16,896]{2,0,1:T(8,128)(2,1)} %copy.128), calls=%async_computation.1 | async-start | bytes 7340032 | tf_op jit(solution)/shard_map/all_to_all | solution.py:48
  58.9 369.5 %reduce-scatter.2.cloned.1.call-start = ((), (), s32[]{:S(2)}) async-start(), calls=%async_computation.3 | async-start | bytes 12386304 | tf_op jit(solution)/shard_map/reduce_scatter | solution.py:74
  65.5 64.6 %collective-permute-start.4 = (bf16[128,4096]{1,0:T(8,128)(2,1)}, bf16[128,4096]{1,0:T(8,128)(2,1)}, u32[]{:S(2)}, u32[]{:S(2)}) collective-permute-start(bf16[128,4096]{1,0:T(8,128)(2,1)} %collective-permute-done.2), channel_id=1, source_target_pairs={{0,1},{1,2},{2,3},{3,4},{4,5},{5,6},{6,7},{7,8},{8,9},{9,10},{10,1... | collective-permute-start | bytes 3145736 | tf_op jit(solution)/shard_map/ppermute | solution.py:57
  71.8 59.9 %collective-permute-start.5 = (bf16[128,4096]{1,0:T(8,128)(2,1)S(1)}, bf16[128,4096]{1,0:T(8,128)(2,1)}, u32[]{:S(2)}, u32[]{:S(2)}) collective-permute-start(bf16[128,4096]{1,0:T(8,128)(2,1)S(1)} %collective-permute-done.3), channel_id=1, source_target_pairs={{0,15},{1,0},{2,1},{3,2},{4,3},{5,4},{6,5},{7,6},{8,7},{9,8},{10,9... | collective-permute-start | bytes 3145736 | tf_op jit(solution)/shard_map/ppermute | solution.py:60
  79.3 58.5 %copy-start.2 = (bf16[128,4096]{1,0:T(8,128)(2,1)S(1)}, bf16[128,4096]{1,0:T(8,128)(2,1)}, u32[]{:S(2)}) copy-start(bf16[128,4096]{1,0:T(8,128)(2,1)} %copy-done.1) | copy-start | bytes 3145732
  130.1 26.7 %collective-permute-start.6 = (bf16[128,4096]{1,0:T(8,128)(2,1)}, bf16[128,4096]{1,0:T(8,128)(2,1)}, u32[]{:S(2)}, u32[]{:S(2)}) collective-permute-start(bf16[128,4096]{1,0:T(8,128)(2,1)} %collective-permute-done.4), channel_id=1, source_target_pairs={{0,1},{1,2},{2,3},{3,4},{4,5},{5,6},{6,7},{7,8},{8,9},{9,10},{10,1... | collective-permute-start | bytes 3145736 | tf_op jit(solution)/shard_map/ppermute | solution.py:57
  131.8 26.8 %collective-permute-start.7 = (bf16[128,4096]{1,0:T(8,128)(2,1)}, bf16[128,4096]{1,0:T(8,128)(2,1)}, u32[]{:S(2)}, u32[]{:S(2)}) collective-permute-start(bf16[128,4096]{1,0:T(8,128)(2,1)} %collective-permute-done.5), channel_id=1, source_target_pairs={{0,15},{1,0},{2,1},{3,2},{4,3},{5,4},{6,5},{7,6},{8,7},{9,8},{10,9... | collective-permute-start | bytes 3145736 | tf_op jit(solution)/shard_map/ppermute | solution.py:60
  156.9 25.8 %collective-permute-start.8 = (bf16[128,4096]{1,0:T(8,128)(2,1)}, bf16[128,4096]{1,0:T(8,128)(2,1)}, u32[]{:S(2)}, u32[]{:S(2)}) collective-permute-start(bf16[128,4096]{1,0:T(8,128)(2,1)} %collective-permute-done.6), channel_id=1, source_target_pairs={{0,1},{1,2},{2,3},{3,4},{4,5},{5,6},{6,7},{7,8},{8,9},{9,10},{10,1... | collective-permute-start | bytes 3145736 | tf_op jit(solution)/shard_map/ppermute | solution.py:57
  158.6 32.8 %collective-permute-start.9 = (bf16[128,4096]{1,0:T(8,128)(2,1)}, bf16[128,4096]{1,0:T(8,128)(2,1)S(1)}, u32[]{:S(2)}, u32[]{:S(2)}) collective-permute-start(bf16[128,4096]{1,0:T(8,128)(2,1)} %collective-permute-done.7), channel_id=1, source_target_pairs={{0,15},{1,0},{2,1},{3,2},{4,3},{5,4},{6,5},{7,6},{8,7},{9,8},{10,9... | collective-permute-start | bytes 3145736 | tf_op jit(solution)/shard_map/ppermute | solution.py:60
  182.7 24.9 %collective-permute-start.10 = (bf16[128,4096]{1,0:T(8,128)(2,1)}, bf16[128,4096]{1,0:T(8,128)(2,1)}, u32[]{:S(2)}, u32[]{:S(2)}) collective-permute-start(bf16[128,4096]{1,0:T(8,128)(2,1)} %collective-permute-done.8), channel_id=1, source_target_pairs={{0,1},{1,2},{2,3},{3,4},{4,5},{5,6},{6,7},{7,8},{8,9},{9,10},{10,1... | collective-permute-start | bytes 3145736 | tf_op jit(solution)/shard_map/ppermute | solution.py:57
  191.4 23.7 %collective-permute-start.11 = (bf16[128,4096]{1,0:T(8,128)(2,1)S(1)}, bf16[128,4096]{1,0:T(8,128)(2,1)}, u32[]{:S(2)}, u32[]{:S(2)}) collective-permute-start(bf16[128,4096]{1,0:T(8,128)(2,1)S(1)} %collective-permute-done.9), channel_id=1, source_target_pairs={{0,15},{1,0},{2,1},{3,2},{4,3},{5,4},{6,5},{7,6},{8,7},{9,8},{10,9... | collective-permute-start | bytes 3145736 | tf_op jit(solution)/shard_map/ppermute | solution.py:60
  207.5 24.0 %collective-permute-start.12 = (bf16[128,4096]{1,0:T(8,128)(2,1)}, bf16[128,4096]{1,0:T(8,128)(2,1)}, u32[]{:S(2)}, u32[]{:S(2)}) collective-permute-start(bf16[128,4096]{1,0:T(8,128)(2,1)} %collective-permute-done.10), channel_id=1, source_target_pairs={{0,1},{1,2},{2,3},{3,4},{4,5},{5,6},{6,7},{7,8},{8,9},{9,10},{10,1... | collective-permute-start | bytes 3145736 | tf_op jit(solution)/shard_map/ppermute | solution.py:57
  215.1 23.8 %collective-permute-start.13 = (bf16[128,4096]{1,0:T(8,128)(2,1)}, bf16[128,4096]{1,0:T(8,128)(2,1)S(1)}, u32[]{:S(2)}, u32[]{:S(2)}) collective-permute-start(bf16[128,4096]{1,0:T(8,128)(2,1)} %collective-permute-done.11), channel_id=1, source_target_pairs={{0,15},{1,0},{2,1},{3,2},{4,3},{5,4},{6,5},{7,6},{8,7},{9,8},{10,9... | collective-permute-start | bytes 3145736 | tf_op jit(solution)/shard_map/ppermute | solution.py:60
  231.5 23.0 %collective-permute-start.14 = (bf16[128,4096]{1,0:T(8,128)(2,1)}, bf16[128,4096]{1,0:T(8,128)(2,1)}, u32[]{:S(2)}, u32[]{:S(2)}) collective-permute-start(bf16[128,4096]{1,0:T(8,128)(2,1)} %collective-permute-done.12), channel_id=1, source_target_pairs={{0,1},{1,2},{2,3},{3,4},{4,5},{5,6},{6,7},{7,8},{8,9},{9,10},{10,1... | collective-permute-start | bytes 3145736 | tf_op jit(solution)/shard_map/ppermute | solution.py:57
Sparse Core Ops, SparseCore 0:
  310.1 118.2 reduce-scatter.1
